TPU v7x, 32 devices: a whole 2x2x4 slice. The times are simulated.
32 devices in a mesh: section: 4 (over z), row: 8 (over y, x, core).
Axes of the slice: x: 2, y: 2, z: 4, core: 2. Of those that a mesh axis runs over, the one named last changes fastest.
Arguments:
- features: bfloat16 [16, 16, 16, 192], P(None, 'row'), may hold values from -6 to 6
- norm_gain: float32 [4, 192], P('section'), may hold values from 0.5 to 1.5
- conv_weight: bfloat16 [4, 3, 3, 3, 192, 192], P('section'), may hold values from -0.078125 to 0.078125
- conv_bias: float32 [4, 192], P('section'), may hold values from -2.5 to 2.5
Outputs:
- decoded: bfloat16 [16, 16, 16, 192], P('section', 'row')
All inputs are finite; a program needn't handle non-finite values.
Results may differ from a plain program's by a relative error of at most 0.03.
Values may be sent and summed in bfloat16 or wider, within the bound.
A program may use at most 64 MiB of HBM per device.

v0:
```python
import jax
import jax.numpy as jnp
from jax import lax
from jax.sharding import PartitionSpec as P

FRAMES = 4


def with_halo(block, sides, width):
    for axis, dim in sides:
        count = lax.axis_size(axis)
        forward = [(i, i + 1) for i in range(count - 1)]
        backward = [(target, source) for source, target in forward]
        low = lax.ppermute(
            lax.slice_in_dim(block, block.shape[dim] - width, None, axis=dim), axis, forward
        )
        high = lax.ppermute(lax.slice_in_dim(block, 0, width, axis=dim), axis, backward)
        block = jnp.concatenate([low, block, high], axis=dim)
    return block


def shifted(value, axis, steps):
    count = lax.axis_size(axis)
    first, last = (max(0, -steps), min(count, count - steps))
    return lax.ppermute(value, axis, [(source, source + steps) for source in range(first, last)])


def on_device(features, norm_gain, conv_weight, conv_bias):
    sections = lax.axis_size("section")
    place = lax.axis_index("section")
    frames_all, rows_dev, cols, chans = features.shape
    group = 2
    span = group * FRAMES
    batches = sections // group
    turns = batches + sections - 1
    blocks = features.reshape(batches, span, rows_dev, cols, chans)
    gain = norm_gain[0]
    bias = conv_bias[0]
    taps = conv_weight[0].reshape(3, 9 * chans, chans)

    def activate(state):
        wide = state.astype(jnp.float32)
        square = jnp.mean(wide * wide, axis=-1, keepdims=True)
        return jax.nn.silu(wide * lax.rsqrt(square + 1e-06) * gain).astype(jnp.bfloat16)

    def convolve(padded, state):
        framed = jnp.pad(padded, ((0, 0), (0, 0), (1, 1), (0, 0)))
        total = jnp.zeros((span * rows_dev * cols, chans), jnp.float32)
        for delay in range(3):
            window = framed[delay : delay + span]
            pieces = [
                window[:, dy : dy + rows_dev, dx : dx + cols] for dy in range(3) for dx in range(3)
            ]
            stacked = jnp.concatenate(pieces, axis=-1).reshape(-1, 9 * chans)
            total = total + jnp.dot(stacked, taps[delay], preferred_element_type=jnp.float32)
        result = state.astype(jnp.float32) + total.reshape(span, rows_dev, cols, chans) + bias
        return result.astype(jnp.bfloat16)

    memory = jnp.zeros((2, rows_dev, cols, chans), jnp.bfloat16)
    incoming = jnp.zeros((span, rows_dev, cols, chans), jnp.bfloat16)
    finished = jnp.zeros((batches, span, rows_dev, cols, chans), jnp.bfloat16)

    def advance(carry, turn):
        incoming, memory, finished = carry
        batch = turn - place
        active = jnp.logical_and(batch >= 0, batch < batches)
        slot = jnp.clip(batch, 0, batches - 1)
        own = lax.dynamic_index_in_dim(blocks, jnp.clip(turn, 0, batches - 1), 0, keepdims=False)
        state = jnp.where(place == 0, own, incoming)
        normed = activate(state)
        joined = jnp.concatenate([memory, normed], axis=0)
        padded = with_halo(joined, (("row", 1),), 1)
        renewed = normed[-2:]
        memory = jnp.where(active, renewed, memory)
        output = lax.cond(active, lambda: convolve(padded, state), lambda: state)
        keeping = jnp.logical_and(active, place == sections - 1)
        finished = jnp.where(
            keeping, lax.dynamic_update_index_in_dim(finished, output, slot, 0), finished
        )
        incoming = shifted(output, "section", 1)
        return ((incoming, memory, finished), None)

    carry, unused = lax.scan(advance, (incoming, memory, finished), jnp.arange(turns))
    finished = carry[2].reshape(sections, 1, FRAMES, rows_dev, cols, chans)
    received = lax.all_to_all(finished, "section", split_axis=0, concat_axis=1, tiled=True)
    return received[0, sections - 1]


def solution(mesh):
    in_specs = (
        P(None, "row", None, None),
        P("section", None),
        P("section", None, None, None, None, None),
        P("section", None),
    )
    out_specs = P("section", "row", None, None)
    return jax.shard_map(
        on_device, mesh=mesh, in_specs=in_specs, out_specs=out_specs, check_vma=False
    )
```

profile of v0, /device:TPU:2, one launch (start us, length us, event | category | flops | bytes accessed | tf_op | source)
XLA Modules:
  0.0 166.4 jit_solution(8224347381871252293)
XLA Ops:
  0.7 140.7 %while.16 = (s32[]{:T(128)}, bf16[8,2,16,192]{3,2,1,0:T(8,128)(2,1)S(1)}, bf16[2,2,16,192]{3,2,1,0:T(8,128)(2,1)}, bf16[2,8,2,16,192]{4,3,2,1,0:T(8,128)(2,1)}, ...) while((s32[]{:T(128)}, ...), condition=%wide.region_4.5_spmd.clone, body=%wide.region_0.4_spmd.clone.sunk | while | flops 510996736 | bytes 19456960 | solution.py:83
  5.2 1.9 %collective-permute-start = (bf16[10,1,16,192]{3,2,1,0:T(8,128)(2,1)S(1)}, bf16[10,1,16,192]{3,2,1,0:T(8,128)(2,1)S(1)}, u32[]{:S(2)}, u32[]{:S(2)}) collective-permute-start(bf16[10,1,16,192]{3,2,1,0:T(8,128)(2,1)S(1)} %get-tuple-element.311), channel_id=1, source_target_pairs={{1,0},{2,1},{3,2},{4,3},{5,4},{6,5},{7,6},{9,8},{10,9},{11,10},{12... | collective-permute-start | bytes 184328 | tf_op jit(solution)/shard_map/while/body/eval_jaxpr/ppermute | solution.py:17
  7.1 2.4 %collective-permute-start.1 = (bf16[10,1,16,192]{3,2,1,0:T(8,128)(2,1)S(1)}, bf16[10,1,16,192]{3,2,1,0:T(8,128)(2,1)S(1)}, u32[]{:S(2)}, u32[]{:S(2)}) collective-permute-start(bf16[10,1,16,192]{3,2,1,0:T(8,128)(2,1)S(1)} %get-tuple-element.312), channel_id=1, source_target_pairs={{0,1},{1,2},{2,3},{3,4},{4,5},{5,6},{6,7},{8,9},{9,10},{10,11},{11... | collective-permute-start | bytes 184328 | tf_op jit(solution)/shard_map/while/body/eval_jaxpr/ppermute | solution.py:14
  9.6 3.3 %collective-permute-done.1 = bf16[10,1,16,192]{3,2,1,0:T(8,128)(2,1)S(1)} collective-permute-done((bf16[10,1,16,192]{3,2,1,0:T(8,128)(2,1)S(1)}, bf16[10,1,16,192]{3,2,1,0:T(8,128)(2,1)S(1)}, u32[]{:S(2)}, u32[]{:S(2)}) %collective-permute-start.1) | collective-permute-done | bytes 61472 | tf_op jit(solution)/shard_map/while/body/eval_jaxpr/ppermute | solution.py:14
  13.0 10.9 %conditional.3 = (bf16[8,2,16,192]{3,2,1,0:T(8,128)(2,1)S(1)}) conditional(s32[]{:T(128)} %convert_element_type.53, bf16[8,2,16,192]{3,2,1,0:T(8,128)(2,1)S(1)} %get-tuple-element.308, (bf16[8,2,16,192]{3,2,1,0:T(8,128)(2,1)S(1)}, bf16[10,4,16,192]{3,2,1,0:T(8,128)(2,1)S(1)}, bf16[3,1728,192]{2,1,0:T(8,128)(2,1)}, f32[1,192]{1,0:T(1,128)}) %tuple.80), branch_computations={%region_2.2_spmd, %region_3.3_spmd} | conditional | flops 509902848 | bytes 16879396 | solution.py:75
  33.7 1.9 %collective-permute-start = (bf16[10,1,16,192]{3,2,1,0:T(8,128)(2,1)S(1)}, bf16[10,1,16,192]{3,2,1,0:T(8,128)(2,1)S(1)}, u32[]{:S(2)}, u32[]{:S(2)}) collective-permute-start(bf16[10,1,16,192]{3,2,1,0:T(8,128)(2,1)S(1)} %get-tuple-element.311), channel_id=1, source_target_pairs={{1,0},{2,1},{3,2},{4,3},{5,4},{6,5},{7,6},{9,8},{10,9},{11,10},{12... | collective-permute-start | bytes 184328 | tf_op jit(solution)/shard_map/while/body/eval_jaxpr/ppermute | solution.py:17
  35.6 2.4 %collective-permute-start.1 = (bf16[10,1,16,192]{3,2,1,0:T(8,128)(2,1)S(1)}, bf16[10,1,16,192]{3,2,1,0:T(8,128)(2,1)S(1)}, u32[]{:S(2)}, u32[]{:S(2)}) collective-permute-start(bf16[10,1,16,192]{3,2,1,0:T(8,128)(2,1)S(1)} %get-tuple-element.312), channel_id=1, source_target_pairs={{0,1},{1,2},{2,3},{3,4},{4,5},{5,6},{6,7},{8,9},{9,10},{10,11},{11... | collective-permute-start | bytes 184328 | tf_op jit(solution)/shard_map/while/body/eval_jaxpr/ppermute | solution.py:14
  38.0 3.3 %collective-permute-done.1 = bf16[10,1,16,192]{3,2,1,0:T(8,128)(2,1)S(1)} collective-permute-done((bf16[10,1,16,192]{3,2,1,0:T(8,128)(2,1)S(1)}, bf16[10,1,16,192]{3,2,1,0:T(8,128)(2,1)S(1)}, u32[]{:S(2)}, u32[]{:S(2)}) %collective-permute-start.1) | collective-permute-done | bytes 61472 | tf_op jit(solution)/shard_map/while/body/eval_jaxpr/ppermute | solution.py:14
  41.4 10.9 %conditional.3 = (bf16[8,2,16,192]{3,2,1,0:T(8,128)(2,1)S(1)}) conditional(s32[]{:T(128)} %convert_element_type.53, bf16[8,2,16,192]{3,2,1,0:T(8,128)(2,1)S(1)} %get-tuple-element.308, (bf16[8,2,16,192]{3,2,1,0:T(8,128)(2,1)S(1)}, bf16[10,4,16,192]{3,2,1,0:T(8,128)(2,1)S(1)}, bf16[3,1728,192]{2,1,0:T(8,128)(2,1)}, f32[1,192]{1,0:T(1,128)}) %tuple.80), branch_computations={%region_2.2_spmd, %region_3.3_spmd} | conditional | flops 509902848 | bytes 16879396 | solution.py:75
  52.3 4.4 %collective-permute-start.2 = (bf16[8,2,16,192]{3,2,1,0:T(8,128)(2,1)S(1)}, bf16[8,2,16,192]{3,2,1,0:T(8,128)(2,1)S(1)}, u32[]{:S(2)}, u32[]{:S(2)}) collective-permute-start(bf16[8,2,16,192]{3,2,1,0:T(8,128)(2,1)S(1)} %get-tuple-element.359), channel_id=1, source_target_pairs={{0,8},{8,16},{16,24},{1,9},{9,17},{17,25},{2,10},{10,18},{18,26},{... | collective-permute-start | bytes 294920 | tf_op jit(solution)/shard_map/while/body/eval_jaxpr/ppermute | solution.py:25
  65.0 1.9 %collective-permute-start = (bf16[10,1,16,192]{3,2,1,0:T(8,128)(2,1)S(1)}, bf16[10,1,16,192]{3,2,1,0:T(8,128)(2,1)S(1)}, u32[]{:S(2)}, u32[]{:S(2)}) collective-permute-start(bf16[10,1,16,192]{3,2,1,0:T(8,128)(2,1)S(1)} %get-tuple-element.311), channel_id=1, source_target_pairs={{1,0},{2,1},{3,2},{4,3},{5,4},{6,5},{7,6},{9,8},{10,9},{11,10},{12... | collective-permute-start | bytes 184328 | tf_op jit(solution)/shard_map/while/body/eval_jaxpr/ppermute | solution.py:17
  66.9 2.4 %collective-permute-start.1 = (bf16[10,1,16,192]{3,2,1,0:T(8,128)(2,1)S(1)}, bf16[10,1,16,192]{3,2,1,0:T(8,128)(2,1)S(1)}, u32[]{:S(2)}, u32[]{:S(2)}) collective-permute-start(bf16[10,1,16,192]{3,2,1,0:T(8,128)(2,1)S(1)} %get-tuple-element.312), channel_id=1, source_target_pairs={{0,1},{1,2},{2,3},{3,4},{4,5},{5,6},{6,7},{8,9},{9,10},{10,11},{11... | collective-permute-start | bytes 184328 | tf_op jit(solution)/shard_map/while/body/eval_jaxpr/ppermute | solution.py:14
  69.4 3.3 %collective-permute-done.1 = bf16[10,1,16,192]{3,2,1,0:T(8,128)(2,1)S(1)} collective-permute-done((bf16[10,1,16,192]{3,2,1,0:T(8,128)(2,1)S(1)}, bf16[10,1,16,192]{3,2,1,0:T(8,128)(2,1)S(1)}, u32[]{:S(2)}, u32[]{:S(2)}) %collective-permute-start.1) | collective-permute-done | bytes 61472 | tf_op jit(solution)/shard_map/while/body/eval_jaxpr/ppermute | solution.py:14
  72.8 15.3 %collective-permute-start.2 = (bf16[8,2,16,192]{3,2,1,0:T(8,128)(2,1)S(1)}, bf16[8,2,16,192]{3,2,1,0:T(8,128)(2,1)S(1)}, u32[]{:S(2)}, u32[]{:S(2)}) collective-permute-start(bf16[8,2,16,192]{3,2,1,0:T(8,128)(2,1)S(1)} %get-tuple-element.359), channel_id=1, source_target_pairs={{0,8},{8,16},{16,24},{1,9},{9,17},{17,25},{2,10},{10,18},{18,26},{... | collective-permute-start | bytes 294920 | tf_op jit(solution)/shard_map/while/body/eval_jaxpr/ppermute | solution.py:25
  96.7 1.9 %collective-permute-start = (bf16[10,1,16,192]{3,2,1,0:T(8,128)(2,1)S(1)}, bf16[10,1,16,192]{3,2,1,0:T(8,128)(2,1)S(1)}, u32[]{:S(2)}, u32[]{:S(2)}) collective-permute-start(bf16[10,1,16,192]{3,2,1,0:T(8,128)(2,1)S(1)} %get-tuple-element.311), channel_id=1, source_target_pairs={{1,0},{2,1},{3,2},{4,3},{5,4},{6,5},{7,6},{9,8},{10,9},{11,10},{12... | collective-permute-start | bytes 184328 | tf_op jit(solution)/shard_map/while/body/eval_jaxpr/ppermute | solution.py:17
  98.6 2.4 %collective-permute-start.1 = (bf16[10,1,16,192]{3,2,1,0:T(8,128)(2,1)S(1)}, bf16[10,1,16,192]{3,2,1,0:T(8,128)(2,1)S(1)}, u32[]{:S(2)}, u32[]{:S(2)}) collective-permute-start(bf16[10,1,16,192]{3,2,1,0:T(8,128)(2,1)S(1)} %get-tuple-element.312), channel_id=1, source_target_pairs={{0,1},{1,2},{2,3},{3,4},{4,5},{5,6},{6,7},{8,9},{9,10},{10,11},{11... | collective-permute-start | bytes 184328 | tf_op jit(solution)/shard_map/while/body/eval_jaxpr/ppermute | solution.py:14
  101.0 3.3 %collective-permute-done.1 = bf16[10,1,16,192]{3,2,1,0:T(8,128)(2,1)S(1)} collective-permute-done((bf16[10,1,16,192]{3,2,1,0:T(8,128)(2,1)S(1)}, bf16[10,1,16,192]{3,2,1,0:T(8,128)(2,1)S(1)}, u32[]{:S(2)}, u32[]{:S(2)}) %collective-permute-start.1) | collective-permute-done | bytes 61472 | tf_op jit(solution)/shard_map/while/body/eval_jaxpr/ppermute | solution.py:14
  104.4 4.4 %collective-permute-start.2 = (bf16[8,2,16,192]{3,2,1,0:T(8,128)(2,1)S(1)}, bf16[8,2,16,192]{3,2,1,0:T(8,128)(2,1)S(1)}, u32[]{:S(2)}, u32[]{:S(2)}) collective-permute-start(bf16[8,2,16,192]{3,2,1,0:T(8,128)(2,1)S(1)} %get-tuple-element.359), channel_id=1, source_target_pairs={{0,8},{8,16},{16,24},{1,9},{9,17},{17,25},{2,10},{10,18},{18,26},{... | collective-permute-start | bytes 294920 | tf_op jit(solution)/shard_map/while/body/eval_jaxpr/ppermute | solution.py:25
  117.4 1.9 %collective-permute-start = (bf16[10,1,16,192]{3,2,1,0:T(8,128)(2,1)S(1)}, bf16[10,1,16,192]{3,2,1,0:T(8,128)(2,1)S(1)}, u32[]{:S(2)}, u32[]{:S(2)}) collective-permute-start(bf16[10,1,16,192]{3,2,1,0:T(8,128)(2,1)S(1)} %get-tuple-element.311), channel_id=1, source_target_pairs={{1,0},{2,1},{3,2},{4,3},{5,4},{6,5},{7,6},{9,8},{10,9},{11,10},{12... | collective-permute-start | bytes 184328 | tf_op jit(solution)/shard_map/while/body/eval_jaxpr/ppermute | solution.py:17
  119.3 2.4 %collective-permute-start.1 = (bf16[10,1,16,192]{3,2,1,0:T(8,128)(2,1)S(1)}, bf16[10,1,16,192]{3,2,1,0:T(8,128)(2,1)S(1)}, u32[]{:S(2)}, u32[]{:S(2)}) collective-permute-start(bf16[10,1,16,192]{3,2,1,0:T(8,128)(2,1)S(1)} %get-tuple-element.312), channel_id=1, source_target_pairs={{0,1},{1,2},{2,3},{3,4},{4,5},{5,6},{6,7},{8,9},{9,10},{10,11},{11... | collective-permute-start | bytes 184328 | tf_op jit(solution)/shard_map/while/body/eval_jaxpr/ppermute | solution.py:14
  121.8 3.3 %collective-permute-done.1 = bf16[10,1,16,192]{3,2,1,0:T(8,128)(2,1)S(1)} collective-permute-done((bf16[10,1,16,192]{3,2,1,0:T(8,128)(2,1)S(1)}, bf16[10,1,16,192]{3,2,1,0:T(8,128)(2,1)S(1)}, u32[]{:S(2)}, u32[]{:S(2)}) %collective-permute-start.1) | collective-permute-done | bytes 61472 | tf_op jit(solution)/shard_map/while/body/eval_jaxpr/ppermute | solution.py:14
  125.2 12.8 %collective-permute-start.2 = (bf16[8,2,16,192]{3,2,1,0:T(8,128)(2,1)S(1)}, bf16[8,2,16,192]{3,2,1,0:T(8,128)(2,1)S(1)}, u32[]{:S(2)}, u32[]{:S(2)}) collective-permute-start(bf16[8,2,16,192]{3,2,1,0:T(8,128)(2,1)S(1)} %get-tuple-element.359), channel_id=1, source_target_pairs={{0,8},{8,16},{16,24},{1,9},{9,17},{17,25},{2,10},{10,18},{18,26},{... | collective-permute-start | bytes 294920 | tf_op jit(solution)/shard_map/while/body/eval_jaxpr/ppermute | solution.py:25
  139.6 1.8 %collective-permute-done.2 = bf16[8,2,16,192]{3,2,1,0:T(8,128)(2,1)S(1)} collective-permute-done((bf16[8,2,16,192]{3,2,1,0:T(8,128)(2,1)S(1)}, bf16[8,2,16,192]{3,2,1,0:T(8,128)(2,1)S(1)}, u32[]{:S(2)}, u32[]{:S(2)}) %collective-permute-start.2) | collective-permute-done | bytes 98336 | tf_op jit(solution)/shard_map/while/body/eval_jaxpr/ppermute | solution.py:25
  141.4 24.3 %all_to_all.12 = bf16[4,1,4,2,16,192]{5,4,3,2,1,0:T(8,128)(2,1)S(1)} all-to-all(bf16[4,1,4,2,16,192]{5,4,3,2,1,0:T(8,128)(2,1)} %bitcast.43), channel_id=1, replica_groups=mesh['section'=4,'row'=8] {'section'}, dimensions={0} | all-to-all | bytes 393216 | tf_op jit(solution)/shard_map/all_to_all | solution.py:85
  (82 shorter events, 58.1 us)
Async XLA Ops:
  5.2 4.4 %collective-permute-start = (bf16[10,1,16,192]{3,2,1,0:T(8,128)(2,1)S(1)}, bf16[10,1,16,192]{3,2,1,0:T(8,128)(2,1)S(1)}, u32[]{:S(2)}, u32[]{:S(2)}) collective-permute-start(bf16[10,1,16,192]{3,2,1,0:T(8,128)(2,1)S(1)} %get-tuple-element.311), channel_id=1, source_target_pairs={{1,0},{2,1},{3,2},{4,3},{5,4},{6,5},{7,6},{9,8},{10,9},{11,10},{12... | collective-permute-start | bytes 184328 | tf_op jit(solution)/shard_map/while/body/eval_jaxpr/ppermute | solution.py:17
  7.1 5.8 %collective-permute-start.1 = (bf16[10,1,16,192]{3,2,1,0:T(8,128)(2,1)S(1)}, bf16[10,1,16,192]{3,2,1,0:T(8,128)(2,1)S(1)}, u32[]{:S(2)}, u32[]{:S(2)}) collective-permute-start(bf16[10,1,16,192]{3,2,1,0:T(8,128)(2,1)S(1)} %get-tuple-element.312), channel_id=1, source_target_pairs={{0,1},{1,2},{2,3},{3,4},{4,5},{5,6},{6,7},{8,9},{9,10},{10,11},{11... | collective-permute-start | bytes 184328 | tf_op jit(solution)/shard_map/while/body/eval_jaxpr/ppermute | solution.py:14
  20.3 3.5 %copy-start = (f32[1,192]{1,0:T(1,128)S(1)}, f32[1,192]{1,0:T(1,128)}, u32[]{:S(2)}) copy-start(f32[1,192]{1,0:T(1,128)} %get-tuple-element.113) | copy-start | bytes 2308 | tf_op jit(solution)/shard_map/while/body/eval_jaxpr/cond
  23.9 4.6 %collective-permute-start.2 = (bf16[8,2,16,192]{3,2,1,0:T(8,128)(2,1)S(1)}, bf16[8,2,16,192]{3,2,1,0:T(8,128)(2,1)S(1)}, u32[]{:S(2)}, u32[]{:S(2)}) collective-permute-start(bf16[8,2,16,192]{3,2,1,0:T(8,128)(2,1)S(1)} %get-tuple-element.359), channel_id=1, source_target_pairs={{0,8},{8,16},{16,24},{1,9},{9,17},{17,25},{2,10},{10,18},{18,26},{... | collective-permute-start | bytes 294920 | tf_op jit(solution)/shard_map/while/body/eval_jaxpr/ppermute | solution.py:25
  33.7 4.4 %collective-permute-start = (bf16[10,1,16,192]{3,2,1,0:T(8,128)(2,1)S(1)}, bf16[10,1,16,192]{3,2,1,0:T(8,128)(2,1)S(1)}, u32[]{:S(2)}, u32[]{:S(2)}) collective-permute-start(bf16[10,1,16,192]{3,2,1,0:T(8,128)(2,1)S(1)} %get-tuple-element.311), channel_id=1, source_target_pairs={{1,0},{2,1},{3,2},{4,3},{5,4},{6,5},{7,6},{9,8},{10,9},{11,10},{12... | collective-permute-start | bytes 184328 | tf_op jit(solution)/shard_map/while/body/eval_jaxpr/ppermute | solution.py:17
  35.6 5.8 %collective-permute-start.1 = (bf16[10,1,16,192]{3,2,1,0:T(8,128)(2,1)S(1)}, bf16[10,1,16,192]{3,2,1,0:T(8,128)(2,1)S(1)}, u32[]{:S(2)}, u32[]{:S(2)}) collective-permute-start(bf16[10,1,16,192]{3,2,1,0:T(8,128)(2,1)S(1)} %get-tuple-element.312), channel_id=1, source_target_pairs={{0,1},{1,2},{2,3},{3,4},{4,5},{5,6},{6,7},{8,9},{9,10},{10,11},{11... | collective-permute-start | bytes 184328 | tf_op jit(solution)/shard_map/while/body/eval_jaxpr/ppermute | solution.py:14
  48.7 3.5 %copy-start = (f32[1,192]{1,0:T(1,128)S(1)}, f32[1,192]{1,0:T(1,128)}, u32[]{:S(2)}) copy-start(f32[1,192]{1,0:T(1,128)} %get-tuple-element.113) | copy-start | bytes 2308 | tf_op jit(solution)/shard_map/while/body/eval_jaxpr/cond
  52.3 7.5 %collective-permute-start.2 = (bf16[8,2,16,192]{3,2,1,0:T(8,128)(2,1)S(1)}, bf16[8,2,16,192]{3,2,1,0:T(8,128)(2,1)S(1)}, u32[]{:S(2)}, u32[]{:S(2)}) collective-permute-start(bf16[8,2,16,192]{3,2,1,0:T(8,128)(2,1)S(1)} %get-tuple-element.359), channel_id=1, source_target_pairs={{0,8},{8,16},{16,24},{1,9},{9,17},{17,25},{2,10},{10,18},{18,26},{... | collective-permute-start | bytes 294920 | tf_op jit(solution)/shard_map/while/body/eval_jaxpr/ppermute | solution.py:25
  65.0 4.4 %collective-permute-start = (bf16[10,1,16,192]{3,2,1,0:T(8,128)(2,1)S(1)}, bf16[10,1,16,192]{3,2,1,0:T(8,128)(2,1)S(1)}, u32[]{:S(2)}, u32[]{:S(2)}) collective-permute-start(bf16[10,1,16,192]{3,2,1,0:T(8,128)(2,1)S(1)} %get-tuple-element.311), channel_id=1, source_target_pairs={{1,0},{2,1},{3,2},{4,3},{5,4},{6,5},{7,6},{9,8},{10,9},{11,10},{12... | collective-permute-start | bytes 184328 | tf_op jit(solution)/shard_map/while/body/eval_jaxpr/ppermute | solution.py:17
  66.9 5.8 %collective-permute-start.1 = (bf16[10,1,16,192]{3,2,1,0:T(8,128)(2,1)S(1)}, bf16[10,1,16,192]{3,2,1,0:T(8,128)(2,1)S(1)}, u32[]{:S(2)}, u32[]{:S(2)}) collective-permute-start(bf16[10,1,16,192]{3,2,1,0:T(8,128)(2,1)S(1)} %get-tuple-element.312), channel_id=1, source_target_pairs={{0,1},{1,2},{2,3},{3,4},{4,5},{5,6},{6,7},{8,9},{9,10},{10,11},{11... | collective-permute-start | bytes 184328 | tf_op jit(solution)/shard_map/while/body/eval_jaxpr/ppermute | solution.py:14
  72.8 18.6 %collective-permute-start.2 = (bf16[8,2,16,192]{3,2,1,0:T(8,128)(2,1)S(1)}, bf16[8,2,16,192]{3,2,1,0:T(8,128)(2,1)S(1)}, u32[]{:S(2)}, u32[]{:S(2)}) collective-permute-start(bf16[8,2,16,192]{3,2,1,0:T(8,128)(2,1)S(1)} %get-tuple-element.359), channel_id=1, source_target_pairs={{0,8},{8,16},{16,24},{1,9},{9,17},{17,25},{2,10},{10,18},{18,26},{... | collective-permute-start | bytes 294920 | tf_op jit(solution)/shard_map/while/body/eval_jaxpr/ppermute | solution.py:25
  96.7 4.4 %collective-permute-start = (bf16[10,1,16,192]{3,2,1,0:T(8,128)(2,1)S(1)}, bf16[10,1,16,192]{3,2,1,0:T(8,128)(2,1)S(1)}, u32[]{:S(2)}, u32[]{:S(2)}) collective-permute-start(bf16[10,1,16,192]{3,2,1,0:T(8,128)(2,1)S(1)} %get-tuple-element.311), channel_id=1, source_target_pairs={{1,0},{2,1},{3,2},{4,3},{5,4},{6,5},{7,6},{9,8},{10,9},{11,10},{12... | collective-permute-start | bytes 184328 | tf_op jit(solution)/shard_map/while/body/eval_jaxpr/ppermute | solution.py:17
  98.6 5.8 %collective-permute-start.1 = (bf16[10,1,16,192]{3,2,1,0:T(8,128)(2,1)S(1)}, bf16[10,1,16,192]{3,2,1,0:T(8,128)(2,1)S(1)}, u32[]{:S(2)}, u32[]{:S(2)}) collective-permute-start(bf16[10,1,16,192]{3,2,1,0:T(8,128)(2,1)S(1)} %get-tuple-element.312), channel_id=1, source_target_pairs={{0,1},{1,2},{2,3},{3,4},{4,5},{5,6},{6,7},{8,9},{9,10},{10,11},{11... | collective-permute-start | bytes 184328 | tf_op jit(solution)/shard_map/while/body/eval_jaxpr/ppermute | solution.py:14
  104.4 7.8 %collective-permute-start.2 = (bf16[8,2,16,192]{3,2,1,0:T(8,128)(2,1)S(1)}, bf16[8,2,16,192]{3,2,1,0:T(8,128)(2,1)S(1)}, u32[]{:S(2)}, u32[]{:S(2)}) collective-permute-start(bf16[8,2,16,192]{3,2,1,0:T(8,128)(2,1)S(1)} %get-tuple-element.359), channel_id=1, source_target_pairs={{0,8},{8,16},{16,24},{1,9},{9,17},{17,25},{2,10},{10,18},{18,26},{... | collective-permute-start | bytes 294920 | tf_op jit(solution)/shard_map/while/body/eval_jaxpr/ppermute | solution.py:25
  117.4 4.4 %collective-permute-start = (bf16[10,1,16,192]{3,2,1,0:T(8,128)(2,1)S(1)}, bf16[10,1,16,192]{3,2,1,0:T(8,128)(2,1)S(1)}, u32[]{:S(2)}, u32[]{:S(2)}) collective-permute-start(bf16[10,1,16,192]{3,2,1,0:T(8,128)(2,1)S(1)} %get-tuple-element.311), channel_id=1, source_target_pairs={{1,0},{2,1},{3,2},{4,3},{5,4},{6,5},{7,6},{9,8},{10,9},{11,10},{12... | collective-permute-start | bytes 184328 | tf_op jit(solution)/shard_map/while/body/eval_jaxpr/ppermute | solution.py:17
  119.3 5.8 %collective-permute-start.1 = (bf16[10,1,16,192]{3,2,1,0:T(8,128)(2,1)S(1)}, bf16[10,1,16,192]{3,2,1,0:T(8,128)(2,1)S(1)}, u32[]{:S(2)}, u32[]{:S(2)}) collective-permute-start(bf16[10,1,16,192]{3,2,1,0:T(8,128)(2,1)S(1)} %get-tuple-element.312), channel_id=1, source_target_pairs={{0,1},{1,2},{2,3},{3,4},{4,5},{5,6},{6,7},{8,9},{9,10},{10,11},{11... | collective-permute-start | bytes 184328 | tf_op jit(solution)/shard_map/while/body/eval_jaxpr/ppermute | solution.py:14
  125.2 16.2 %collective-permute-start.2 = (bf16[8,2,16,192]{3,2,1,0:T(8,128)(2,1)S(1)}, bf16[8,2,16,192]{3,2,1,0:T(8,128)(2,1)S(1)}, u32[]{:S(2)}, u32[]{:S(2)}) collective-permute-start(bf16[8,2,16,192]{3,2,1,0:T(8,128)(2,1)S(1)} %get-tuple-element.359), channel_id=1, source_target_pairs={{0,8},{8,16},{16,24},{1,9},{9,17},{17,25},{2,10},{10,18},{18,26},{... | collective-permute-start | bytes 294920 | tf_op jit(solution)/shard_map/while/body/eval_jaxpr/ppermute | solution.py:25
where the time goes:
time: 168 us; the launch traced here: 166 us
  starting transfers between devices  59.8 us (36%)
  waiting for transfers between devices  25.1 us (15%)
  blocking collectives  24.3 us (14%)
  other arithmetic  24.1 us (14%)
  local copies, waits for them, and re-layouts  15.8 us (9%)
  matrix products  10.1 us (6%)
  loops' own time  7.08 us (4%)
    ppermute x5, starting transfers between devices, shifted(): lax.ppermute(value, axis, [(source, source + steps) for source in range(f...  38.2 us
    all_to_all x1, blocking collectives, on_device(): lax.all_to_all(finished, 'section', split_axis=0, concat_axis=1, tiled=True)  24.3 us
    ppermute x5, waiting for transfers between devices, with_halo(): lax.ppermute(lax.slice_in_dim(block, block.shape[dim] - width, None, axis...  16.6 us
    ppermute x5, starting transfers between devices, with_halo(): lax.ppermute(lax.slice_in_dim(block, block.shape[dim] - width, None, axis...  12 us
    dot_general x6, matrix products, convolve(): jnp.dot(stacked, taps[delay], preferred_element_type=jnp.float32)  10.1 us
    ppermute x5, starting transfers between devices, with_halo(): lax.ppermute(lax.slice_in_dim(block, 0, width, axis=dim), axis, backward)  9.6 us
    ppermute x5, waiting for transfers between devices, shifted(): lax.ppermute(value, axis, [(source, source + steps) for source in range(f...  8.46 us
    concatenate x6, local copies, waits for them, and re-layouts, convolve(): stacked = jnp.concatenate(pieces, axis=-1).reshape(-1, 9 * chans)  8.15 us
  transfers between devices with their start and end apart: 15, of which 10 were waited for; matrix products, arithmetic and copies ran while one was open for 5% of the time, Pallas kernels for 0%

commit v1 on v0

--- a/solution.py
+++ b/solution.py
@@ -2,8 +2,23 @@
 import jax.numpy as jnp
 from jax import lax
 from jax.sharding import PartitionSpec as P
+from jax.lax import axis_index, axis_size, ppermute
 
 FRAMES = 4
+
+
+def cells_time(raw, axis_no, arr_in):
+    w1 = raw.shape
+    mid_arr = raw.reshape(*w1[:axis_no], arr_in, w1[axis_no] // arr_in, *w1[axis_no + 1 :])
+    return jnp.moveaxis(mid_arr, axis_no, 0)
+
+
+def _read_arrays(local_block, on_dim):
+    local_block = jnp.moveaxis(local_block, 0, on_dim)
+    m_next = local_block.shape
+    return local_block.reshape(
+        *m_next[:on_dim], m_next[on_dim] * m_next[on_dim + 1], *m_next[on_dim + 2 :]
+    )
 
 
 def with_halo(block, sides, width):
@@ -82,7 +97,14 @@
 
     carry, unused = lax.scan(advance, (incoming, memory, finished), jnp.arange(turns))
     finished = carry[2].reshape(sections, 1, FRAMES, rows_dev, cols, chans)
-    received = lax.all_to_all(finished, "section", split_axis=0, concat_axis=1, tiled=True)
+    upper, res = (axis_size("section"), axis_index("section"))
+    reply = cells_time(finished, 0, upper)
+    pages = [reply[res]]
+    for ix in range(1, upper):
+        now = reply[res ^ ix]
+        pages.append(ppermute(now, "section", [(t, t ^ ix) for t in range(upper)]))
+    reply = jnp.stack(pages)[res ^ jnp.arange(upper)]
+    received = _read_arrays(reply, 1)
     return received[0, sections - 1]
 
 

time: 168 us -> 160 us (0.952)
  blocking collectives: 24.3 us -> 0 us
  starting transfers between devices: 59.8 us -> 74.9 us
  other arithmetic: 24.1 us -> 18.1 us
  waiting for transfers between devices: 25.1 us -> 29.8 us
    all_to_all x1 -> x0, blocking collectives: 24.3 us -> none  [on_device(): lax.all_to_all(finished, 'section', split_axis=0, concat_axis=1, tiled=True)]
    ppermute x0 -> x3, starting transfers between devices: none -> 15.3 us  [on_device(): pages.append(ppermute(now, 'section', [(t, t ^ ix) for t in range(upper)]))]
    select_n x5, other arithmetic: 6.2 us -> 0.09 us  [advance(): memory = jnp.where(active, renewed, memory)]
    ppermute x0 -> x3, waiting for transfers between devices: none -> 4.69 us  [on_device(): pages.append(ppermute(now, 'section', [(t, t ^ ix) for t in range(upper)]))]
  transfers between devices with their start and end apart: 15 -> 18, of which waited for: 10 -> 13; matrix products, arithmetic and copies ran while one was open for 5% -> 5% of each run, Pallas kernels for 0% -> 0%
where the time goes in v1:
time: 160 us; the launch traced here: 157 us
  starting transfers between devices  74.9 us (47%)
  waiting for transfers between devices  29.8 us (19%)
  other arithmetic  18.1 us (11%)
  local copies, waits for them, and re-layouts  17.1 us (11%)
  matrix products  10.1 us (6%)
  loops' own time  7.07 us (4%)
    ppermute x5, starting transfers between devices, shifted(): lax.ppermute(value, axis, [(source, source + steps) for source in range(f...  38 us
    ppermute x5, waiting for transfers between devices, with_halo(): lax.ppermute(lax.slice_in_dim(block, block.shape[dim] - width, None, axis...  16.6 us
    ppermute x3, starting transfers between devices, on_device(): pages.append(ppermute(now, 'section', [(t, t ^ ix) for t in range(upper)]))  15.3 us
    ppermute x5, starting transfers between devices, with_halo(): lax.ppermute(lax.slice_in_dim(block, block.shape[dim] - width, None, axis...  12 us
    dot_general x6, matrix products, convolve(): jnp.dot(stacked, taps[delay], preferred_element_type=jnp.float32)  10.1 us
    ppermute x5, starting transfers between devices, with_halo(): lax.ppermute(lax.slice_in_dim(block, 0, width, axis=dim), axis, backward)  9.6 us
    ppermute x5, waiting for transfers between devices, shifted(): lax.ppermute(value, axis, [(source, source + steps) for source in range(f...  8.51 us
    select_n x5, other arithmetic, advance(): jnp.where(keeping, lax.dynamic_update_index_in_dim(finished, output, slot...  7.95 us
  transfers between devices with their start and end apart: 18, of which 13 were waited for; matrix products, arithmetic and copies ran while one was open for 5% of the time, Pallas kernels for 0%

profile of v1, /device:TPU:2, one launch (start us, length us, event | category | flops | bytes accessed | tf_op | source)
XLA Modules:
  0.0 157.2 jit_solution(6671306234099605103)
XLA Ops:
  0.7 134.2 %while.16 = (s32[]{:T(128)}, bf16[8,2,16,192]{3,2,1,0:T(8,128)(2,1)S(1)}, bf16[2,2,16,192]{3,2,1,0:T(8,128)(2,1)S(1)}, bf16[2,8,2,16,192]{4,3,2,1,0:T(8,128)(2,1...) while((s32[]{:T(128)}, ...), condition=%wide.region_4.5_spmd.clone, body=%wide.region_0.4_spmd.clone.sunk | while | flops 510996736 | bytes 19456960 | solution.py:98
  4.6 1.9 %collective-permute-start = (bf16[10,1,16,192]{3,2,1,0:T(8,128)(2,1)S(1)}, bf16[10,1,16,192]{3,2,1,0:T(8,128)(2,1)S(1)}, u32[]{:S(2)}, u32[]{:S(2)}) collective-permute-start(bf16[10,1,16,192]{3,2,1,0:T(8,128)(2,1)S(1)} %get-tuple-element.315), channel_id=1, source_target_pairs={{1,0},{2,1},{3,2},{4,3},{5,4},{6,5},{7,6},{9,8},{10,9},{11,10},{12... | collective-permute-start | bytes 184328 | tf_op jit(solution)/shard_map/while/body/eval_jaxpr/ppermute | solution.py:32
  6.5 2.4 %collective-permute-start.1 = (bf16[10,1,16,192]{3,2,1,0:T(8,128)(2,1)S(1)}, bf16[10,1,16,192]{3,2,1,0:T(8,128)(2,1)S(1)}, u32[]{:S(2)}, u32[]{:S(2)}) collective-permute-start(bf16[10,1,16,192]{3,2,1,0:T(8,128)(2,1)S(1)} %get-tuple-element.316), channel_id=1, source_target_pairs={{0,1},{1,2},{2,3},{3,4},{4,5},{5,6},{6,7},{8,9},{9,10},{10,11},{11... | collective-permute-start | bytes 184328 | tf_op jit(solution)/shard_map/while/body/eval_jaxpr/ppermute | solution.py:29
  9.0 3.3 %collective-permute-done.1 = bf16[10,1,16,192]{3,2,1,0:T(8,128)(2,1)S(1)} collective-permute-done((bf16[10,1,16,192]{3,2,1,0:T(8,128)(2,1)S(1)}, bf16[10,1,16,192]{3,2,1,0:T(8,128)(2,1)S(1)}, u32[]{:S(2)}, u32[]{:S(2)}) %collective-permute-start.1) | collective-permute-done | bytes 61472 | tf_op jit(solution)/shard_map/while/body/eval_jaxpr/ppermute | solution.py:29
  12.4 10.8 %conditional.3 = (bf16[8,2,16,192]{3,2,1,0:T(8,128)(2,1)S(1)}) conditional(s32[]{:T(128)} %convert_element_type.53, bf16[8,2,16,192]{3,2,1,0:T(8,128)(2,1)S(1)} %get-tuple-element.312, (bf16[8,2,16,192]{3,2,1,0:T(8,128)(2,1)S(1)}, bf16[10,4,16,192]{3,2,1,0:T(8,128)(2,1)S(1)}, bf16[3,1728,192]{2,1,0:T(8,128)(2,1)}, f32[1,192]{1,0:T(1,128)}) %tuple.83), branch_computations={%region_2.2_spmd, %region_3.3_spmd} | conditional | flops 509902848 | bytes 16879396 | solution.py:90
  31.6 1.9 %collective-permute-start = (bf16[10,1,16,192]{3,2,1,0:T(8,128)(2,1)S(1)}, bf16[10,1,16,192]{3,2,1,0:T(8,128)(2,1)S(1)}, u32[]{:S(2)}, u32[]{:S(2)}) collective-permute-start(bf16[10,1,16,192]{3,2,1,0:T(8,128)(2,1)S(1)} %get-tuple-element.315), channel_id=1, source_target_pairs={{1,0},{2,1},{3,2},{4,3},{5,4},{6,5},{7,6},{9,8},{10,9},{11,10},{12... | collective-permute-start | bytes 184328 | tf_op jit(solution)/shard_map/while/body/eval_jaxpr/ppermute | solution.py:32
  33.5 2.4 %collective-permute-start.1 = (bf16[10,1,16,192]{3,2,1,0:T(8,128)(2,1)S(1)}, bf16[10,1,16,192]{3,2,1,0:T(8,128)(2,1)S(1)}, u32[]{:S(2)}, u32[]{:S(2)}) collective-permute-start(bf16[10,1,16,192]{3,2,1,0:T(8,128)(2,1)S(1)} %get-tuple-element.316), channel_id=1, source_target_pairs={{0,1},{1,2},{2,3},{3,4},{4,5},{5,6},{6,7},{8,9},{9,10},{10,11},{11... | collective-permute-start | bytes 184328 | tf_op jit(solution)/shard_map/while/body/eval_jaxpr/ppermute | solution.py:29
  35.9 3.3 %collective-permute-done.1 = bf16[10,1,16,192]{3,2,1,0:T(8,128)(2,1)S(1)} collective-permute-done((bf16[10,1,16,192]{3,2,1,0:T(8,128)(2,1)S(1)}, bf16[10,1,16,192]{3,2,1,0:T(8,128)(2,1)S(1)}, u32[]{:S(2)}, u32[]{:S(2)}) %collective-permute-start.1) | collective-permute-done | bytes 61472 | tf_op jit(solution)/shard_map/while/body/eval_jaxpr/ppermute | solution.py:29
  39.3 10.8 %conditional.3 = (bf16[8,2,16,192]{3,2,1,0:T(8,128)(2,1)S(1)}) conditional(s32[]{:T(128)} %convert_element_type.53, bf16[8,2,16,192]{3,2,1,0:T(8,128)(2,1)S(1)} %get-tuple-element.312, (bf16[8,2,16,192]{3,2,1,0:T(8,128)(2,1)S(1)}, bf16[10,4,16,192]{3,2,1,0:T(8,128)(2,1)S(1)}, bf16[3,1728,192]{2,1,0:T(8,128)(2,1)}, f32[1,192]{1,0:T(1,128)}) %tuple.83), branch_computations={%region_2.2_spmd, %region_3.3_spmd} | conditional | flops 509902848 | bytes 16879396 | solution.py:90
  50.1 4.4 %collective-permute-start.2 = (bf16[8,2,16,192]{3,2,1,0:T(8,128)(2,1)S(1)}, bf16[8,2,16,192]{3,2,1,0:T(8,128)(2,1)S(1)}, u32[]{:S(2)}, u32[]{:S(2)}) collective-permute-start(bf16[8,2,16,192]{3,2,1,0:T(8,128)(2,1)S(1)} %get-tuple-element.363), channel_id=1, source_target_pairs={{0,8},{8,16},{16,24},{1,9},{9,17},{17,25},{2,10},{10,18},{18,26},{... | collective-permute-start | bytes 294920 | tf_op jit(solution)/shard_map/while/body/eval_jaxpr/ppermute | solution.py:40
  61.5 1.9 %collective-permute-start = (bf16[10,1,16,192]{3,2,1,0:T(8,128)(2,1)S(1)}, bf16[10,1,16,192]{3,2,1,0:T(8,128)(2,1)S(1)}, u32[]{:S(2)}, u32[]{:S(2)}) collective-permute-start(bf16[10,1,16,192]{3,2,1,0:T(8,128)(2,1)S(1)} %get-tuple-element.315), channel_id=1, source_target_pairs={{1,0},{2,1},{3,2},{4,3},{5,4},{6,5},{7,6},{9,8},{10,9},{11,10},{12... | collective-permute-start | bytes 184328 | tf_op jit(solution)/shard_map/while/body/eval_jaxpr/ppermute | solution.py:32
  63.4 2.4 %collective-permute-start.1 = (bf16[10,1,16,192]{3,2,1,0:T(8,128)(2,1)S(1)}, bf16[10,1,16,192]{3,2,1,0:T(8,128)(2,1)S(1)}, u32[]{:S(2)}, u32[]{:S(2)}) collective-permute-start(bf16[10,1,16,192]{3,2,1,0:T(8,128)(2,1)S(1)} %get-tuple-element.316), channel_id=1, source_target_pairs={{0,1},{1,2},{2,3},{3,4},{4,5},{5,6},{6,7},{8,9},{9,10},{10,11},{11... | collective-permute-start | bytes 184328 | tf_op jit(solution)/shard_map/while/body/eval_jaxpr/ppermute | solution.py:29
  65.8 3.3 %collective-permute-done.1 = bf16[10,1,16,192]{3,2,1,0:T(8,128)(2,1)S(1)} collective-permute-done((bf16[10,1,16,192]{3,2,1,0:T(8,128)(2,1)S(1)}, bf16[10,1,16,192]{3,2,1,0:T(8,128)(2,1)S(1)}, u32[]{:S(2)}, u32[]{:S(2)}) %collective-permute-start.1) | collective-permute-done | bytes 61472 | tf_op jit(solution)/shard_map/while/body/eval_jaxpr/ppermute | solution.py:29
  69.2 15.2 %collective-permute-start.2 = (bf16[8,2,16,192]{3,2,1,0:T(8,128)(2,1)S(1)}, bf16[8,2,16,192]{3,2,1,0:T(8,128)(2,1)S(1)}, u32[]{:S(2)}, u32[]{:S(2)}) collective-permute-start(bf16[8,2,16,192]{3,2,1,0:T(8,128)(2,1)S(1)} %get-tuple-element.363), channel_id=1, source_target_pairs={{0,8},{8,16},{16,24},{1,9},{9,17},{17,25},{2,10},{10,18},{18,26},{... | collective-permute-start | bytes 294920 | tf_op jit(solution)/shard_map/while/body/eval_jaxpr/ppermute | solution.py:40
  91.6 1.9 %collective-permute-start = (bf16[10,1,16,192]{3,2,1,0:T(8,128)(2,1)S(1)}, bf16[10,1,16,192]{3,2,1,0:T(8,128)(2,1)S(1)}, u32[]{:S(2)}, u32[]{:S(2)}) collective-permute-start(bf16[10,1,16,192]{3,2,1,0:T(8,128)(2,1)S(1)} %get-tuple-element.315), channel_id=1, source_target_pairs={{1,0},{2,1},{3,2},{4,3},{5,4},{6,5},{7,6},{9,8},{10,9},{11,10},{12... | collective-permute-start | bytes 184328 | tf_op jit(solution)/shard_map/while/body/eval_jaxpr/ppermute | solution.py:32
  93.6 2.4 %collective-permute-start.1 = (bf16[10,1,16,192]{3,2,1,0:T(8,128)(2,1)S(1)}, bf16[10,1,16,192]{3,2,1,0:T(8,128)(2,1)S(1)}, u32[]{:S(2)}, u32[]{:S(2)}) collective-permute-start(bf16[10,1,16,192]{3,2,1,0:T(8,128)(2,1)S(1)} %get-tuple-element.316), channel_id=1, source_target_pairs={{0,1},{1,2},{2,3},{3,4},{4,5},{5,6},{6,7},{8,9},{9,10},{10,11},{11... | collective-permute-start | bytes 184328 | tf_op jit(solution)/shard_map/while/body/eval_jaxpr/ppermute | solution.py:29
  96.0 3.3 %collective-permute-done.1 = bf16[10,1,16,192]{3,2,1,0:T(8,128)(2,1)S(1)} collective-permute-done((bf16[10,1,16,192]{3,2,1,0:T(8,128)(2,1)S(1)}, bf16[10,1,16,192]{3,2,1,0:T(8,128)(2,1)S(1)}, u32[]{:S(2)}, u32[]{:S(2)}) %collective-permute-start.1) | collective-permute-done | bytes 61472 | tf_op jit(solution)/shard_map/while/body/eval_jaxpr/ppermute | solution.py:29
  99.4 4.4 %collective-permute-start.2 = (bf16[8,2,16,192]{3,2,1,0:T(8,128)(2,1)S(1)}, bf16[8,2,16,192]{3,2,1,0:T(8,128)(2,1)S(1)}, u32[]{:S(2)}, u32[]{:S(2)}) collective-permute-start(bf16[8,2,16,192]{3,2,1,0:T(8,128)(2,1)S(1)} %get-tuple-element.363), channel_id=1, source_target_pairs={{0,8},{8,16},{16,24},{1,9},{9,17},{17,25},{2,10},{10,18},{18,26},{... | collective-permute-start | bytes 294920 | tf_op jit(solution)/shard_map/while/body/eval_jaxpr/ppermute | solution.py:40
  111.0 1.9 %collective-permute-start = (bf16[10,1,16,192]{3,2,1,0:T(8,128)(2,1)S(1)}, bf16[10,1,16,192]{3,2,1,0:T(8,128)(2,1)S(1)}, u32[]{:S(2)}, u32[]{:S(2)}) collective-permute-start(bf16[10,1,16,192]{3,2,1,0:T(8,128)(2,1)S(1)} %get-tuple-element.315), channel_id=1, source_target_pairs={{1,0},{2,1},{3,2},{4,3},{5,4},{6,5},{7,6},{9,8},{10,9},{11,10},{12... | collective-permute-start | bytes 184328 | tf_op jit(solution)/shard_map/while/body/eval_jaxpr/ppermute | solution.py:32
  113.0 2.4 %collective-permute-start.1 = (bf16[10,1,16,192]{3,2,1,0:T(8,128)(2,1)S(1)}, bf16[10,1,16,192]{3,2,1,0:T(8,128)(2,1)S(1)}, u32[]{:S(2)}, u32[]{:S(2)}) collective-permute-start(bf16[10,1,16,192]{3,2,1,0:T(8,128)(2,1)S(1)} %get-tuple-element.316), channel_id=1, source_target_pairs={{0,1},{1,2},{2,3},{3,4},{4,5},{5,6},{6,7},{8,9},{9,10},{10,11},{11... | collective-permute-start | bytes 184328 | tf_op jit(solution)/shard_map/while/body/eval_jaxpr/ppermute | solution.py:29
  115.4 3.3 %collective-permute-done.1 = bf16[10,1,16,192]{3,2,1,0:T(8,128)(2,1)S(1)} collective-permute-done((bf16[10,1,16,192]{3,2,1,0:T(8,128)(2,1)S(1)}, bf16[10,1,16,192]{3,2,1,0:T(8,128)(2,1)S(1)}, u32[]{:S(2)}, u32[]{:S(2)}) %collective-permute-start.1) | collective-permute-done | bytes 61472 | tf_op jit(solution)/shard_map/while/body/eval_jaxpr/ppermute | solution.py:29
  118.8 12.7 %collective-permute-start.2 = (bf16[8,2,16,192]{3,2,1,0:T(8,128)(2,1)S(1)}, bf16[8,2,16,192]{3,2,1,0:T(8,128)(2,1)S(1)}, u32[]{:S(2)}, u32[]{:S(2)}) collective-permute-start(bf16[8,2,16,192]{3,2,1,0:T(8,128)(2,1)S(1)} %get-tuple-element.363), channel_id=1, source_target_pairs={{0,8},{8,16},{16,24},{1,9},{9,17},{17,25},{2,10},{10,18},{18,26},{... | collective-permute-start | bytes 294920 | tf_op jit(solution)/shard_map/while/body/eval_jaxpr/ppermute | solution.py:40
  135.9 14.7 %collective-permute-start.5 = (bf16[1,1,4,2,16,192]{5,4,3,2,1,0:T(8,128)(2,1)S(1)}, bf16[1,1,4,2,16,192]{5,4,3,2,1,0:T(8,128)(2,1)S(1)}, u32[]{:S(2)}, u32[]{:S(2)}) collective-permute-start(bf16[1,1,4,2,16,192]{5,4,3,2,1,0:T(8,128)(2,1)S(1)} %get-tuple-element.230), channel_id=1, source_target_pairs={{0,24},{8,16},{16,8},{24,0},{1,25},{9,17},{17,9},{25,1},{2,26},{10... | collective-permute-start | bytes 147464 | tf_op jit(solution)/shard_map/ppermute | solution.py:105
  153.1 2.7 %collective-permute-done.4 = bf16[1,1,4,2,16,192]{5,4,3,2,1,0:T(8,128)(2,1)S(1)} collective-permute-done((bf16[1,1,4,2,16,192]{5,4,3,2,1,0:T(8,128)(2,1)S(1)}, bf16[1,1,4,2,16,192]{5,4,3,2,1,0:T(8,128)(2,1)S(1)}, u32[]{:S(2)}, u32[]{:S(2)}) %collective-permute-start.4) | collective-permute-done | bytes 49184 | tf_op jit(solution)/shard_map/ppermute | solution.py:105
  (92 shorter events, 57.8 us)
Async XLA Ops:
  4.6 4.4 %collective-permute-start = (bf16[10,1,16,192]{3,2,1,0:T(8,128)(2,1)S(1)}, bf16[10,1,16,192]{3,2,1,0:T(8,128)(2,1)S(1)}, u32[]{:S(2)}, u32[]{:S(2)}) collective-permute-start(bf16[10,1,16,192]{3,2,1,0:T(8,128)(2,1)S(1)} %get-tuple-element.315), channel_id=1, source_target_pairs={{1,0},{2,1},{3,2},{4,3},{5,4},{6,5},{7,6},{9,8},{10,9},{11,10},{12... | collective-permute-start | bytes 184328 | tf_op jit(solution)/shard_map/while/body/eval_jaxpr/ppermute | solution.py:32
  6.5 5.8 %collective-permute-start.1 = (bf16[10,1,16,192]{3,2,1,0:T(8,128)(2,1)S(1)}, bf16[10,1,16,192]{3,2,1,0:T(8,128)(2,1)S(1)}, u32[]{:S(2)}, u32[]{:S(2)}) collective-permute-start(bf16[10,1,16,192]{3,2,1,0:T(8,128)(2,1)S(1)} %get-tuple-element.316), channel_id=1, source_target_pairs={{0,1},{1,2},{2,3},{3,4},{4,5},{5,6},{6,7},{8,9},{9,10},{10,11},{11... | collective-permute-start | bytes 184328 | tf_op jit(solution)/shard_map/while/body/eval_jaxpr/ppermute | solution.py:29
  20.7 2.4 %copy-start = (f32[1,192]{1,0:T(1,128)S(1)}, f32[1,192]{1,0:T(1,128)}, u32[]{:S(2)}) copy-start(f32[1,192]{1,0:T(1,128)} %get-tuple-element.113) | copy-start | bytes 2308 | tf_op jit(solution)/shard_map/while/body/eval_jaxpr/cond
  23.2 4.6 %collective-permute-start.2 = (bf16[8,2,16,192]{3,2,1,0:T(8,128)(2,1)S(1)}, bf16[8,2,16,192]{3,2,1,0:T(8,128)(2,1)S(1)}, u32[]{:S(2)}, u32[]{:S(2)}) collective-permute-start(bf16[8,2,16,192]{3,2,1,0:T(8,128)(2,1)S(1)} %get-tuple-element.363), channel_id=1, source_target_pairs={{0,8},{8,16},{16,24},{1,9},{9,17},{17,25},{2,10},{10,18},{18,26},{... | collective-permute-start | bytes 294920 | tf_op jit(solution)/shard_map/while/body/eval_jaxpr/ppermute | solution.py:40
  31.6 4.4 %collective-permute-start = (bf16[10,1,16,192]{3,2,1,0:T(8,128)(2,1)S(1)}, bf16[10,1,16,192]{3,2,1,0:T(8,128)(2,1)S(1)}, u32[]{:S(2)}, u32[]{:S(2)}) collective-permute-start(bf16[10,1,16,192]{3,2,1,0:T(8,128)(2,1)S(1)} %get-tuple-element.315), channel_id=1, source_target_pairs={{1,0},{2,1},{3,2},{4,3},{5,4},{6,5},{7,6},{9,8},{10,9},{11,10},{12... | collective-permute-start | bytes 184328 | tf_op jit(solution)/shard_map/while/body/eval_jaxpr/ppermute | solution.py:32
  33.5 5.8 %collective-permute-start.1 = (bf16[10,1,16,192]{3,2,1,0:T(8,128)(2,1)S(1)}, bf16[10,1,16,192]{3,2,1,0:T(8,128)(2,1)S(1)}, u32[]{:S(2)}, u32[]{:S(2)}) collective-permute-start(bf16[10,1,16,192]{3,2,1,0:T(8,128)(2,1)S(1)} %get-tuple-element.316), channel_id=1, source_target_pairs={{0,1},{1,2},{2,3},{3,4},{4,5},{5,6},{6,7},{8,9},{9,10},{10,11},{11... | collective-permute-start | bytes 184328 | tf_op jit(solution)/shard_map/while/body/eval_jaxpr/ppermute | solution.py:29
  47.7 2.4 %copy-start = (f32[1,192]{1,0:T(1,128)S(1)}, f32[1,192]{1,0:T(1,128)}, u32[]{:S(2)}) copy-start(f32[1,192]{1,0:T(1,128)} %get-tuple-element.113) | copy-start | bytes 2308 | tf_op jit(solution)/shard_map/while/body/eval_jaxpr/cond
  50.1 7.5 %collective-permute-start.2 = (bf16[8,2,16,192]{3,2,1,0:T(8,128)(2,1)S(1)}, bf16[8,2,16,192]{3,2,1,0:T(8,128)(2,1)S(1)}, u32[]{:S(2)}, u32[]{:S(2)}) collective-permute-start(bf16[8,2,16,192]{3,2,1,0:T(8,128)(2,1)S(1)} %get-tuple-element.363), channel_id=1, source_target_pairs={{0,8},{8,16},{16,24},{1,9},{9,17},{17,25},{2,10},{10,18},{18,26},{... | collective-permute-start | bytes 294920 | tf_op jit(solution)/shard_map/while/body/eval_jaxpr/ppermute | solution.py:40
  61.5 4.4 %collective-permute-start = (bf16[10,1,16,192]{3,2,1,0:T(8,128)(2,1)S(1)}, bf16[10,1,16,192]{3,2,1,0:T(8,128)(2,1)S(1)}, u32[]{:S(2)}, u32[]{:S(2)}) collective-permute-start(bf16[10,1,16,192]{3,2,1,0:T(8,128)(2,1)S(1)} %get-tuple-element.315), channel_id=1, source_target_pairs={{1,0},{2,1},{3,2},{4,3},{5,4},{6,5},{7,6},{9,8},{10,9},{11,10},{12... | collective-permute-start | bytes 184328 | tf_op jit(solution)/shard_map/while/body/eval_jaxpr/ppermute | solution.py:32
  63.4 5.8 %collective-permute-start.1 = (bf16[10,1,16,192]{3,2,1,0:T(8,128)(2,1)S(1)}, bf16[10,1,16,192]{3,2,1,0:T(8,128)(2,1)S(1)}, u32[]{:S(2)}, u32[]{:S(2)}) collective-permute-start(bf16[10,1,16,192]{3,2,1,0:T(8,128)(2,1)S(1)} %get-tuple-element.316), channel_id=1, source_target_pairs={{0,1},{1,2},{2,3},{3,4},{4,5},{5,6},{6,7},{8,9},{9,10},{10,11},{11... | collective-permute-start | bytes 184328 | tf_op jit(solution)/shard_map/while/body/eval_jaxpr/ppermute | solution.py:29
  69.2 18.5 %collective-permute-start.2 = (bf16[8,2,16,192]{3,2,1,0:T(8,128)(2,1)S(1)}, bf16[8,2,16,192]{3,2,1,0:T(8,128)(2,1)S(1)}, u32[]{:S(2)}, u32[]{:S(2)}) collective-permute-start(bf16[8,2,16,192]{3,2,1,0:T(8,128)(2,1)S(1)} %get-tuple-element.363), channel_id=1, source_target_pairs={{0,8},{8,16},{16,24},{1,9},{9,17},{17,25},{2,10},{10,18},{18,26},{... | collective-permute-start | bytes 294920 | tf_op jit(solution)/shard_map/while/body/eval_jaxpr/ppermute | solution.py:40
  91.6 4.4 %collective-permute-start = (bf16[10,1,16,192]{3,2,1,0:T(8,128)(2,1)S(1)}, bf16[10,1,16,192]{3,2,1,0:T(8,128)(2,1)S(1)}, u32[]{:S(2)}, u32[]{:S(2)}) collective-permute-start(bf16[10,1,16,192]{3,2,1,0:T(8,128)(2,1)S(1)} %get-tuple-element.315), channel_id=1, source_target_pairs={{1,0},{2,1},{3,2},{4,3},{5,4},{6,5},{7,6},{9,8},{10,9},{11,10},{12... | collective-permute-start | bytes 184328 | tf_op jit(solution)/shard_map/while/body/eval_jaxpr/ppermute | solution.py:32
  93.6 5.8 %collective-permute-start.1 = (bf16[10,1,16,192]{3,2,1,0:T(8,128)(2,1)S(1)}, bf16[10,1,16,192]{3,2,1,0:T(8,128)(2,1)S(1)}, u32[]{:S(2)}, u32[]{:S(2)}) collective-permute-start(bf16[10,1,16,192]{3,2,1,0:T(8,128)(2,1)S(1)} %get-tuple-element.316), channel_id=1, source_target_pairs={{0,1},{1,2},{2,3},{3,4},{4,5},{5,6},{6,7},{8,9},{9,10},{10,11},{11... | collective-permute-start | bytes 184328 | tf_op jit(solution)/shard_map/while/body/eval_jaxpr/ppermute | solution.py:29
  99.4 7.8 %collective-permute-start.2 = (bf16[8,2,16,192]{3,2,1,0:T(8,128)(2,1)S(1)}, bf16[8,2,16,192]{3,2,1,0:T(8,128)(2,1)S(1)}, u32[]{:S(2)}, u32[]{:S(2)}) collective-permute-start(bf16[8,2,16,192]{3,2,1,0:T(8,128)(2,1)S(1)} %get-tuple-element.363), channel_id=1, source_target_pairs={{0,8},{8,16},{16,24},{1,9},{9,17},{17,25},{2,10},{10,18},{18,26},{... | collective-permute-start | bytes 294920 | tf_op jit(solution)/shard_map/while/body/eval_jaxpr/ppermute | solution.py:40
  111.0 4.4 %collective-permute-start = (bf16[10,1,16,192]{3,2,1,0:T(8,128)(2,1)S(1)}, bf16[10,1,16,192]{3,2,1,0:T(8,128)(2,1)S(1)}, u32[]{:S(2)}, u32[]{:S(2)}) collective-permute-start(bf16[10,1,16,192]{3,2,1,0:T(8,128)(2,1)S(1)} %get-tuple-element.315), channel_id=1, source_target_pairs={{1,0},{2,1},{3,2},{4,3},{5,4},{6,5},{7,6},{9,8},{10,9},{11,10},{12... | collective-permute-start | bytes 184328 | tf_op jit(solution)/shard_map/while/body/eval_jaxpr/ppermute | solution.py:32
  113.0 5.8 %collective-permute-start.1 = (bf16[10,1,16,192]{3,2,1,0:T(8,128)(2,1)S(1)}, bf16[10,1,16,192]{3,2,1,0:T(8,128)(2,1)S(1)}, u32[]{:S(2)}, u32[]{:S(2)}) collective-permute-start(bf16[10,1,16,192]{3,2,1,0:T(8,128)(2,1)S(1)} %get-tuple-element.316), channel_id=1, source_target_pairs={{0,1},{1,2},{2,3},{3,4},{4,5},{5,6},{6,7},{8,9},{9,10},{10,11},{11... | collective-permute-start | bytes 184328 | tf_op jit(solution)/shard_map/while/body/eval_jaxpr/ppermute | solution.py:29
  118.8 16.1 %collective-permute-start.2 = (bf16[8,2,16,192]{3,2,1,0:T(8,128)(2,1)S(1)}, bf16[8,2,16,192]{3,2,1,0:T(8,128)(2,1)S(1)}, u32[]{:S(2)}, u32[]{:S(2)}) collective-permute-start(bf16[8,2,16,192]{3,2,1,0:T(8,128)(2,1)S(1)} %get-tuple-element.363), channel_id=1, source_target_pairs={{0,8},{8,16},{16,24},{1,9},{9,17},{17,25},{2,10},{10,18},{18,26},{... | collective-permute-start | bytes 294920 | tf_op jit(solution)/shard_map/while/body/eval_jaxpr/ppermute | solution.py:40
  135.9 17.2 %collective-permute-start.5 = (bf16[1,1,4,2,16,192]{5,4,3,2,1,0:T(8,128)(2,1)S(1)}, bf16[1,1,4,2,16,192]{5,4,3,2,1,0:T(8,128)(2,1)S(1)}, u32[]{:S(2)}, u32[]{:S(2)}) collective-permute-start(bf16[1,1,4,2,16,192]{5,4,3,2,1,0:T(8,128)(2,1)S(1)} %get-tuple-element.230), channel_id=1, source_target_pairs={{0,24},{8,16},{16,8},{24,0},{1,25},{9,17},{17,9},{25,1},{2,26},{10... | collective-permute-start | bytes 147464 | tf_op jit(solution)/shard_map/ppermute | solution.py:105
  150.5 5.3 %collective-permute-start.4 = (bf16[1,1,4,2,16,192]{5,4,3,2,1,0:T(8,128)(2,1)S(1)}, bf16[1,1,4,2,16,192]{5,4,3,2,1,0:T(8,128)(2,1)S(1)}, u32[]{:S(2)}, u32[]{:S(2)}) collective-permute-start(bf16[1,1,4,2,16,192]{5,4,3,2,1,0:T(8,128)(2,1)S(1)} %get-tuple-element.231), channel_id=1, source_target_pairs={{0,16},{8,24},{16,0},{24,8},{1,17},{9,25},{17,1},{25,9},{2,18},{10... | collective-permute-start | bytes 147464 | tf_op jit(solution)/shard_map/ppermute | solution.py:105
  150.5 5.3 %collective-permute-start.3 = (bf16[1,1,4,2,16,192]{5,4,3,2,1,0:T(8,128)(2,1)S(1)}, bf16[1,1,4,2,16,192]{5,4,3,2,1,0:T(8,128)(2,1)S(1)}, u32[]{:S(2)}, u32[]{:S(2)}) collective-permute-start(bf16[1,1,4,2,16,192]{5,4,3,2,1,0:T(8,128)(2,1)S(1)} %get-tuple-element.232), channel_id=1, source_target_pairs={{0,8},{8,0},{16,24},{24,16},{1,9},{9,1},{17,25},{25,17},{2,10},{10... | collective-permute-start | bytes 147464 | tf_op jit(solution)/shard_map/ppermute | solution.py:105
